TPU v7x, 512 devices: a whole 4x8x8 slice. The times are simulated.
512 devices in a mesh: tm: 32 (over y, z_lo), row: 16 (over x, z_hi, core).
Axes of the slice: x: 4, y: 8, z: 8 (z_hi: 2, z_lo: 4; z = z_hi * 4 + z_lo), core: 2. Of those that a mesh axis runs over, the one named last changes fastest.
Arguments:
- latents: bfloat16 [64, 96, 80, 256], P('tm', 'row'), may hold values from -6 to 6
- conv_weight: bfloat16 [3, 3, 768, 256], replicated, may hold values from -0.078125 to 0.078125
- norm_gain: float32 [256], replicated, may hold values from 0.1 to 1.9
- depth_target: bfloat16 [64, 96, 80, 128], P('tm', 'row'), may hold values from -6 to 6
Outputs:
- features: bfloat16 [64, 96, 80, 256], P('tm', 'row')
- gram: float32 [256, 256], replicated
- cross: float32 [256, 128], replicated
All inputs are finite; a program needn't handle non-finite values.
Results may differ from a plain program's by a relative error of at most 0.003.
Values may be sent and summed in bfloat16 or wider, within the bound.
A program may use at most 64 MiB of HBM per device.

v0:
```python
import jax
import jax.numpy as jnp
from jax import lax
from jax.sharding import PartitionSpec as P


def from_behind(value, axis, steps):
    count = lax.axis_size(axis)
    first, last = (max(0, -steps), min(count, count - steps))
    return lax.ppermute(value, axis, [(source, source + steps) for source in range(first, last)])


def extended(cells, sides, width):
    for axis, dim in sides:
        count = lax.axis_size(axis)
        ends = count - 1
        head = lax.slice_in_dim(cells, 0, width, axis=dim)
        tail = lax.slice_in_dim(cells, cells.shape[dim] - width, cells.shape[dim], axis=dim)
        cells = jnp.concatenate(
            [
                lax.ppermute(tail, axis, [(i, (i + 1) % count) for i in range(ends)]),
                cells,
                lax.ppermute(head, axis, [((i + 1) % count, i) for i in range(ends)]),
            ],
            axis=dim,
        )
    return cells


def convolve(padded, conv_weight):
    frames = padded.shape[0] - 2
    rows = padded.shape[1] - 2
    cols = padded.shape[2]
    chans = conv_weight.shape[3]
    wide = jnp.pad(padded, ((0, 0), (0, 0), (1, 1), (0, 0)))
    stacked = jnp.concatenate(
        [wide[:, :, 0:cols], wide[:, :, 1 : cols + 1], wide[:, :, 2 : cols + 2]], axis=3
    )
    total = jnp.zeros((frames * rows * cols, chans), jnp.float32)
    for dtime in range(3):
        for drow in range(3):
            piece = stacked[dtime : dtime + frames, drow : drow + rows].reshape(
                frames * rows * cols, -1
            )
            total = total + jnp.dot(
                piece, conv_weight[dtime, drow], preferred_element_type=jnp.float32
            )
    return total


def on_device(latents, conv_weight, norm_gain, depth_target):
    cached = from_behind(latents, "tm", 1)
    joined = jnp.concatenate([cached, latents], axis=0)
    padded = extended(joined, (("row", 1),), 1)
    conv = convolve(padded, conv_weight)
    flat_in = latents.reshape(conv.shape[0], conv.shape[1]).astype(jnp.float32)
    normed = conv * jax.lax.rsqrt(jnp.mean(conv * conv, axis=1, keepdims=True) + 1e-06) * norm_gain
    flat = (flat_in + jax.nn.silu(normed)).astype(jnp.bfloat16)
    targets = depth_target.reshape(flat.shape[0], -1)
    gram_part = jnp.dot(flat.T, flat, preferred_element_type=jnp.float32)
    cross_part = jnp.dot(flat.T, targets, preferred_element_type=jnp.float32)
    count = flat.shape[0] * lax.axis_size("tm") * lax.axis_size("row")
    gram_sum, cross_sum = lax.psum((gram_part, cross_part), ("tm", "row"))
    return (flat.reshape(latents.shape), gram_sum / count, cross_sum / count)


def solution(mesh):
    in_specs = (P("tm", "row", None, None), P(), P(), P("tm", "row", None, None))
    out_specs = (P("tm", "row", None, None), P(), P())
    return jax.shard_map(
        on_device, mesh=mesh, in_specs=in_specs, out_specs=out_specs, check_vma=False
    )
```

profile of v0, /device:TPU:1, one launch (start us, length us, event | category | flops | bytes accessed | tf_op | source)
XLA Modules:
  0.0 338.9 jit_solution(941491397047165075)
XLA Ops:
  7.2 0.0 copy-start
  7.2 0.0 all-reduce.4.cloned.1.call-start
  7.2 5.0 %collective-permute-start = (bf16[2,6,80,256]{3,2,1,0:T(8,128)(2,1)}, bf16[2,6,80,256]{3,2,1,0:T(8,128)(2,1)S(1)}, u32[]{:S(2)}, u32[]{:S(2)}) collective-permute-start(bf16[2,6,80,256]{3,2,1,0:T(8,128)(2,1)} %param.4), channel_id=1, source_target_pairs={{0,16},{16,32},{32,48},{48,64},{64,80},{80,96},{96,112},{112,128},... | collective-permute-start | bytes 1474568 | tf_op jit(solution)/shard_map/ppermute | solution.py:10
  12.2 7.8 %collective-permute-done = bf16[2,6,80,256]{3,2,1,0:T(8,128)(2,1)S(1)} collective-permute-done((bf16[2,6,80,256]{3,2,1,0:T(8,128)(2,1)}, bf16[2,6,80,256]{3,2,1,0:T(8,128)(2,1)S(1)}, u32[]{:S(2)}, u32[]{:S(2)}) %collective-permute-start) | collective-permute-done | bytes 491552 | tf_op jit(solution)/shard_map/ppermute | solution.py:10
  20.1 1.1 constant_dynamic-update-slice_fusion
  21.2 13.5 %collective-permute-start.1 = (bf16[4,1,80,256]{3,2,1,0:T(8,128)(2,1)S(1)}, bf16[4,1,80,256]{3,2,1,0:T(8,128)(2,1)S(1)}, u32[]{:S(2)}, u32[]{:S(2)}) collective-permute-start(bf16[4,1,80,256]{3,2,1,0:T(8,128)(2,1)S(1)} %get-tuple-element.16), channel_id=1, source_target_pairs={{0,1},{1,2},{2,3},{3,4},{4,5},{5,6},{6,7},{7,8},{8,9},{9,10},{10,1... | collective-permute-start | bytes 491528 | tf_op jit(solution)/shard_map/ppermute | solution.py:21
  34.7 1.9 collective-permute-start.2
  36.6 2.1 collective-permute-done.1
  38.7 7.3 %collective-permute-done.2 = bf16[4,1,80,256]{3,2,1,0:T(8,128)(2,1)S(1)} collective-permute-done((bf16[4,1,80,256]{3,2,1,0:T(8,128)(2,1)S(1)}, bf16[4,1,80,256]{3,2,1,0:T(8,128)(2,1)S(1)}, u32[]{:S(2)}, u32[]{:S(2)}) %collective-permute-start.2) | collective-permute-done | bytes 163872 | tf_op jit(solution)/shard_map/ppermute | solution.py:23
  46.0 0.8 fusion.5
  46.7 0.9 fusion.41
  47.6 0.3 pad_maximum_fusion
  48.0 0.0 copy-start.1
  48.0 1.2 fusion.40
  49.2 0.7 copy-done.1
  50.0 0.5 fusion.14
  50.5 0.5 fusion.16
  51.1 0.5 fusion.18
  51.6 0.5 fusion.20
  52.2 0.5 fusion.22
  52.8 0.5 fusion.24
  53.3 0.5 fusion.26
  53.9 0.5 fusion.28
  54.4 0.0 copy-start.2
  54.4 0.0 copy-start.4
  54.5 0.9 multiply_reduce_fusion
  55.4 0.1 copy-done.2
  55.5 0.0 copy-done.4
  55.5 0.4 fusion.13
  55.9 0.0 copy-start.3
  55.9 1.1 fusion.43
  56.9 0.0 copy-done
  56.9 1.0 fusion.44
  57.9 0.0 all-reduce.4.cloned.1.call-update
  58.0 270.9 %all-reduce.4.cloned.1.call-done = (f32[256,256]{1,0:T(8,128)}, f32[256,128]{1,0:T(8,128)}) async-done(((f32[256,256]{1,0:T(8,128)}, f32[256,128]{1,0:T(8,128)}), (f32[256,256]{1,0:T(8,128)}, f32[256,128]{1,0:T(8,128)})) %all-reduce.4.cloned.1.call-update) | async-done | bytes 393232 | tf_op jit(solution)/shard_map/psum | solution.py:63
  328.8 1.7 broadcast_multiply_fusion
  330.5 0.0 copy-done.3
  330.5 1.6 broadcast_multiply_fusion.1
  (3 shorter events, 0.1 us)
Async XLA Ops:
  7.2 49.8 %copy-start = (bf16[2,6,80,128]{3,2,1,0:T(8,128)(2,1)S(1)}, bf16[2,6,80,128]{3,2,1,0:T(8,128)(2,1)}, u32[]{:S(2)}) copy-start(bf16[2,6,80,128]{3,2,1,0:T(8,128)(2,1)} %param.7) | copy-start | bytes 737284
  7.2 321.6 %all-reduce.4.cloned.1.call-start = ((), (), s32[]{:S(2)}) async-start(), calls=%async_computation | async-start | bytes 786432 | tf_op jit(solution)/shard_map/psum | solution.py:63
  7.2 12.8 %collective-permute-start = (bf16[2,6,80,256]{3,2,1,0:T(8,128)(2,1)}, bf16[2,6,80,256]{3,2,1,0:T(8,128)(2,1)S(1)}, u32[]{:S(2)}, u32[]{:S(2)}) collective-permute-start(bf16[2,6,80,256]{3,2,1,0:T(8,128)(2,1)} %param.4), channel_id=1, source_target_pairs={{0,16},{16,32},{32,48},{48,64},{64,80},{80,96},{96,112},{112,128},... | collective-permute-start | bytes 1474568 | tf_op jit(solution)/shard_map/ppermute | solution.py:10
  21.2 17.5 %collective-permute-start.1 = (bf16[4,1,80,256]{3,2,1,0:T(8,128)(2,1)S(1)}, bf16[4,1,80,256]{3,2,1,0:T(8,128)(2,1)S(1)}, u32[]{:S(2)}, u32[]{:S(2)}) collective-permute-start(bf16[4,1,80,256]{3,2,1,0:T(8,128)(2,1)S(1)} %get-tuple-element.16), channel_id=1, source_target_pairs={{0,1},{1,2},{2,3},{3,4},{4,5},{5,6},{6,7},{7,8},{8,9},{9,10},{10,1... | collective-permute-start | bytes 491528 | tf_op jit(solution)/shard_map/ppermute | solution.py:21
  34.7 11.3 %collective-permute-start.2 = (bf16[4,1,80,256]{3,2,1,0:T(8,128)(2,1)S(1)}, bf16[4,1,80,256]{3,2,1,0:T(8,128)(2,1)S(1)}, u32[]{:S(2)}, u32[]{:S(2)}) collective-permute-start(bf16[4,1,80,256]{3,2,1,0:T(8,128)(2,1)S(1)} %get-tuple-element.17), channel_id=1, source_target_pairs={{1,0},{2,1},{3,2},{4,3},{5,4},{6,5},{7,6},{8,7},{9,8},{10,9},{11,1... | collective-permute-start | bytes 491528 | tf_op jit(solution)/shard_map/ppermute | solution.py:23
  48.0 2.0 copy-start.1
  54.4 1.0 copy-start.2
  54.4 1.0 copy-start.4
  55.9 274.6 %copy-start.3 = (bf16[960,256]{1,0:T(8,128)(2,1)}, bf16[960,256]{1,0:T(8,128)(2,1)S(1)}, u32[]{:S(2)}) copy-start(bf16[960,256]{1,0:T(8,128)(2,1)S(1)} %fusion.13) | copy-start | bytes 1474564
Sparse Core Ops, SparseCore 0:
  58.1 270.6 all-reduce.3
where the time goes:
time: 339 us
  waiting for transfers between devices  288 us (85%)
  starting transfers between devices  20.4 us (6%)
  between operations  14.2 us (4%)
  matrix products  7.34 us (2%)
  other arithmetic  4.74 us (1%)
  local copies, waits for them, and re-layouts  4.12 us (1%)
    psum x1, waiting for transfers between devices, on_device(): gram_sum, cross_sum = lax.psum((gram_part, cross_part), ('tm', 'row'))  271 us
    ppermute x1, starting transfers between devices, extended(): lax.ppermute(tail, axis, [(i, (i + 1) % count) for i in range(ends)])  13.5 us
    ppermute x1, waiting for transfers between devices, from_behind(): lax.ppermute(value, axis, [(source, source + steps) for source in range(f...  7.81 us
    ppermute x1, waiting for transfers between devices, extended(): lax.ppermute(head, axis, [((i + 1) % count, i) for i in range(ends)])  7.3 us
  transfers between devices with their start and end apart: 4, of which 4 were waited for; matrix products, arithmetic and copies ran while one was open for 0% of the time, Pallas kernels for 0%

commit v1 on v0

--- a/solution.py
+++ b/solution.py
@@ -60,7 +60,7 @@
     gram_part = jnp.dot(flat.T, flat, preferred_element_type=jnp.float32)
     cross_part = jnp.dot(flat.T, targets, preferred_element_type=jnp.float32)
     count = flat.shape[0] * lax.axis_size("tm") * lax.axis_size("row")
-    gram_sum, cross_sum = lax.psum((gram_part, cross_part), ("tm", "row"))
+    gram_sum, cross_sum = lax.psum(lax.psum((gram_part, cross_part), "row"), "tm")
     return (flat.reshape(latents.shape), gram_sum / count, cross_sum / count)
 
 

time: 339 us -> 556 us (1.64)
  the two profiles are of different devices: /device:TPU:1 before, /device:TPU:2 now
where the time goes in v1:
time: 556 us
  waiting for transfers between devices  510 us (92%)
  starting transfers between devices  15 us (3%)
  between operations  14.2 us (3%)
  matrix products  7.34 us (1%)
    psum x1, waiting for transfers between devices, on_device(): lax.psum(lax.psum((gram_part, cross_part), 'row'), 'tm')  313 us
    psum x1, waiting for transfers between devices, on_device(): lax.psum((gram_part, cross_part), 'row')  181 us
  transfers between devices with their start and end apart: 5, of which 5 were waited for; matrix products, arithmetic and copies ran while one was open for 0% of the time, Pallas kernels for 0%

profile of v1, /device:TPU:2, one launch (start us, length us, event | category | flops | bytes accessed | tf_op | source)
XLA Modules:
  0.0 555.6 jit_solution(13335660412421570100)
XLA Ops:
  7.2 0.0 copy-start
  7.2 0.0 all-reduce.8.cloned.1.call-start
  7.2 4.4 collective-permute-start
  11.7 10.7 %collective-permute-done = bf16[2,6,80,256]{3,2,1,0:T(8,128)(2,1)S(1)} collective-permute-done((bf16[2,6,80,256]{3,2,1,0:T(8,128)(2,1)}, bf16[2,6,80,256]{3,2,1,0:T(8,128)(2,1)S(1)}, u32[]{:S(2)}, u32[]{:S(2)}) %collective-permute-start) | collective-permute-done | bytes 491552 | tf_op jit(solution)/shard_map/ppermute | solution.py:10
  22.5 1.1 constant_dynamic-update-slice_fusion
  23.6 1.9 collective-permute-start.1
  25.5 8.6 %collective-permute-start.2 = (bf16[4,1,80,256]{3,2,1,0:T(8,128)(2,1)S(1)}, bf16[4,1,80,256]{3,2,1,0:T(8,128)(2,1)S(1)}, u32[]{:S(2)}, u32[]{:S(2)}) collective-permute-start(bf16[4,1,80,256]{3,2,1,0:T(8,128)(2,1)S(1)} %get-tuple-element.19), channel_id=1, source_target_pairs={{1,0},{2,1},{3,2},{4,3},{5,4},{6,5},{7,6},{8,7},{9,8},{10,9},{11,1... | collective-permute-start | bytes 491528 | tf_op jit(solution)/shard_map/ppermute | solution.py:23
  34.1 1.1 collective-permute-done.1
  35.1 4.2 collective-permute-done.2
  39.3 0.8 fusion.5
  40.1 0.9 fusion.41
  41.0 0.3 pad_maximum_fusion
  41.3 0.0 copy-start.1
  41.3 1.2 fusion.40
  42.6 0.7 copy-done.1
  43.3 0.5 fusion.14
  43.9 0.5 fusion.16
  44.4 0.5 fusion.18
  45.0 0.5 fusion.20
  45.6 0.5 fusion.22
  46.1 0.5 fusion.24
  46.7 0.5 fusion.26
  47.2 0.5 fusion.28
  47.8 0.0 copy-start.2
  47.8 0.0 copy-start.4
  47.8 0.9 multiply_reduce_fusion
  48.7 0.1 copy-done.2
  48.8 0.0 copy-done.4
  48.8 0.4 fusion.13
  49.2 0.0 copy-start.3
  49.2 1.0 fusion.43
  50.3 0.0 copy-done
  50.3 1.0 fusion.44
  51.3 0.0 all-reduce.8.cloned.1.call-update
  51.3 0.0 all-reduce.6.cloned.1.call-start
  51.4 181.0 %all-reduce.8.cloned.1.call-done = (f32[256,256]{1,0:T(8,128)}, f32[256,128]{1,0:T(8,128)}) async-done(((f32[256,256]{1,0:T(8,128)}, f32[256,128]{1,0:T(8,128)}), (f32[256,256]{1,0:T(8,128)}, f32[256,128]{1,0:T(8,128)})) %all-reduce.8.cloned.1.call-update) | async-done | bytes 393232 | tf_op jit(solution)/shard_map/psum | solution.py:63
  232.4 0.0 all-reduce.6.cloned.1.call-update
  232.4 313.1 %all-reduce.6.cloned.1.call-done = (f32[256,256]{1,0:T(8,128)}, f32[256,128]{1,0:T(8,128)}) async-done(((f32[256,256]{1,0:T(8,128)}, f32[256,128]{1,0:T(8,128)}), (f32[256,256]{1,0:T(8,128)}, f32[256,128]{1,0:T(8,128)})) %all-reduce.6.cloned.1.call-update) | async-done | bytes 393232 | tf_op jit(solution)/shard_map/psum | solution.py:63
  545.5 1.7 broadcast_multiply_fusion
  547.2 0.0 copy-done.3
  547.2 1.6 broadcast_multiply_fusion.1
  (3 shorter events, 0.1 us)
Async XLA Ops:
  7.2 43.1 %copy-start = (bf16[2,6,80,128]{3,2,1,0:T(8,128)(2,1)S(1)}, bf16[2,6,80,128]{3,2,1,0:T(8,128)(2,1)}, u32[]{:S(2)}) copy-start(bf16[2,6,80,128]{3,2,1,0:T(8,128)(2,1)} %param.7) | copy-start | bytes 737284
  7.2 225.2 %all-reduce.8.cloned.1.call-start = ((), (), s32[]{:S(2)}) async-start(), calls=%async_computation.1 | async-start | bytes 786432 | tf_op jit(solution)/shard_map/psum | solution.py:63
  7.2 15.2 %collective-permute-start = (bf16[2,6,80,256]{3,2,1,0:T(8,128)(2,1)}, bf16[2,6,80,256]{3,2,1,0:T(8,128)(2,1)S(1)}, u32[]{:S(2)}, u32[]{:S(2)}) collective-permute-start(bf16[2,6,80,256]{3,2,1,0:T(8,128)(2,1)} %param.4), channel_id=1, source_target_pairs={{0,16},{16,32},{32,48},{48,64},{64,80},{80,96},{96,112},{112,128},... | collective-permute-start | bytes 1474568 | tf_op jit(solution)/shard_map/ppermute | solution.py:10
  23.6 11.6 %collective-permute-start.1 = (bf16[4,1,80,256]{3,2,1,0:T(8,128)(2,1)S(1)}, bf16[4,1,80,256]{3,2,1,0:T(8,128)(2,1)S(1)}, u32[]{:S(2)}, u32[]{:S(2)}) collective-permute-start(bf16[4,1,80,256]{3,2,1,0:T(8,128)(2,1)S(1)} %get-tuple-element.18), channel_id=1, source_target_pairs={{0,1},{1,2},{2,3},{3,4},{4,5},{5,6},{6,7},{7,8},{8,9},{9,10},{10,1... | collective-permute-start | bytes 491528 | tf_op jit(solution)/shard_map/ppermute | solution.py:21
  25.5 13.8 %collective-permute-start.2 = (bf16[4,1,80,256]{3,2,1,0:T(8,128)(2,1)S(1)}, bf16[4,1,80,256]{3,2,1,0:T(8,128)(2,1)S(1)}, u32[]{:S(2)}, u32[]{:S(2)}) collective-permute-start(bf16[4,1,80,256]{3,2,1,0:T(8,128)(2,1)S(1)} %get-tuple-element.19), channel_id=1, source_target_pairs={{1,0},{2,1},{3,2},{4,3},{5,4},{6,5},{7,6},{8,7},{9,8},{10,9},{11,1... | collective-permute-start | bytes 491528 | tf_op jit(solution)/shard_map/ppermute | solution.py:23
  41.3 2.0 copy-start.1
  47.8 1.0 copy-start.2
  47.8 1.0 copy-start.4
  49.2 498.0 %copy-start.3 = (bf16[960,256]{1,0:T(8,128)(2,1)}, bf16[960,256]{1,0:T(8,128)(2,1)S(1)}, u32[]{:S(2)}) copy-start(bf16[960,256]{1,0:T(8,128)(2,1)S(1)} %fusion.13) | copy-start | bytes 1474564
  51.3 494.2 %all-reduce.6.cloned.1.call-start = ((), (), s32[]{:S(2)}) async-start(), calls=%async_computation | async-start | bytes 786432 | tf_op jit(solution)/shard_map/psum | solution.py:63
Sparse Core Ops, SparseCore 0:
  51.4 180.9 all-reduce.7
  235.4 310.0 all-reduce.5
